TPU v7x, 32 devices: a whole 2x2x4 slice. The times are simulated.
32 devices in a mesh: tok: 8 (over z, x), tp: 4 (over y, core).
Axes of the slice: x: 2, y: 2, z: 4, core: 2. Of those that a mesh axis runs over, the one named last changes fastest.
Arguments:
- tokens: bfloat16 [36928, 768], P('tok'), may hold values from -6 to 6
- slot_index: int32 [36928], P('tok'), may hold values from -1 to 18477, as said below
- segment: int32 [36928], P('tok'), may hold values from 0 to 3, as said below
- router: float32 [768], replicated, may hold values from -0.21875 to 0.21875
- first_norm: float32 [2, 768], replicated, may hold values from -0.6 to 1.3
- qkv_weight: bfloat16 [768, 3, 768], P(None, None, 'tp'), may hold values from -0.21875 to 0.21875
- qv_bias: float32 [2, 768], P(None, 'tp'), may hold values from -4 to 4
- out_weight: bfloat16 [768, 768], P('tp'), may hold values from -1.75 to 1.75
- out_bias: float32 [768], P('tp'), may hold values from -4 to 4
- second_norm: float32 [2, 768], replicated, may hold values from -0.6 to 1.3
- up_weight: bfloat16 [768, 3072], P(None, 'tp'), may hold values from -0.21875 to 0.21875
- up_bias: float32 [3072], P('tp'), may hold values from -4 to 4
- down_weight: bfloat16 [3072, 768], P('tp'), may hold values from -0.109375 to 0.109375
- down_bias: float32 [768], P('tp'), may hold values from -4 to 4
- cotangent: bfloat16 [36928, 768], P('tok'), may hold values from -6 to 6
Outputs:
- layer_out: bfloat16 [36928, 768], P('tok', 'tp')
- d_tokens: float32 [36928, 768], P('tok', 'tp')
- d_qkv_weight: float32 [768, 3, 768], P(None, None, 'tp')
- d_qv_bias: float32 [2, 768], P(None, 'tp')
- d_out_weight: float32 [768, 768], P('tp')
- d_out_bias: float32 [768], P('tp')
- d_up_weight: float32 [768, 3072], P(None, 'tp')
- d_up_bias: float32 [3072], P('tp')
- d_down_weight: float32 [3072, 768], P('tp')
- d_down_bias: float32 [768], P('tp')
- d_first_norm: float32 [2, 768], P(None, 'tp')
- d_second_norm: float32 [2, 768], P(None, 'tp')
- d_router: float32 [768], P('tp')
Inputs may be any that keep to these rules, and one draw needn't show every extreme that they name: `slot_index`: -1 where the router leaves a patch out; else a slot of the compact buffers, slot // 289 being its row buffer, owned by index slot // 2312 of tok. No slot is named twice, each buffer's named slots are its lowest ones, every index of tok holds exactly 2168 selected patches and owns 2168 named slots, and at most 271 of the selected patches of one index of tok lie in rows of one owner. `segment`: within a row buffer the segments of named slots never fall from one slot to the next.
All inputs are finite; a program needn't handle non-finite values.
Results may differ from a plain program's by a relative error of at most 0.013.
Values may be sent and summed in bfloat16 or wider, within the bound.
No kernel may reach another device: no remote copies, remote signals or barrier semaphores. Data moves between devices by JAX's collectives and lax.ppermute only.
A program may use at most 320 MiB of HBM per device.

v0:
```python
import jax
import jax.numpy as jnp
from jax import lax
from jax.sharding import PartitionSpec as P

HD = 64
ROWS_DEV = 8
SLOTS = 289
EPSILON = 1e-06
MASKED_SCORE = -1000000000.0
BF = jnp.bfloat16
F32 = jnp.float32
EXACT = lax.Precision.HIGHEST


def ceil_to(value, step):
    return -(-value // step) * step


def normal_parts(values):
    row_mean = jnp.mean(values, axis=-1, keepdims=True)
    centered = values - row_mean
    inverse = lax.rsqrt(jnp.mean(centered * centered, axis=-1, keepdims=True) + EPSILON)
    return (centered * inverse, inverse)


def norm_back(grad_in, normal, inverse, gain_row):
    scaled = grad_in * gain_row
    return inverse * (
        scaled
        - jnp.mean(scaled, axis=-1, keepdims=True)
        - normal * jnp.mean(scaled * normal, axis=-1, keepdims=True)
    )


def mul(left, right):
    return lax.dot_general(left, right, (((1,), (0,)), ((), ())), preferred_element_type=F32)


def mul_t0(left, right):
    return lax.dot_general(left, right, (((0,), (0,)), ((), ())), preferred_element_type=F32)


def mul_t1(left, right):
    return lax.dot_general(left, right, (((1,), (1,)), ((), ())), preferred_element_type=F32)


def hot(rows, cols):
    return (rows[:, None] == cols[None, :]).astype(BF)


def columns_of(source, part, shares):
    width = source.shape[-1] // shares
    return lax.dynamic_slice_in_dim(source, part * width, width, source.ndim - 1)


def body(
    tokens,
    slot_index,
    segment,
    router,
    first_norm,
    qkv_weight,
    qv_bias,
    out_weight,
    out_bias,
    second_norm,
    up_weight,
    up_bias,
    down_weight,
    down_bias,
    cotangent,
):
    peers = lax.axis_size("tok")
    shares = lax.axis_size("tp")
    part = lax.axis_index("tp")
    half_bit = part % 2
    pair_bit = part // 2
    half_swap = [(i, i ^ 1) for i in range(shares)]
    pair_swap = [(i, i ^ 2) for i in range(shares)]
    count, width = tokens.shape
    inner = qkv_weight.shape[2]
    heads_local = inner // HD
    owned = ROWS_DEV * SLOTS
    live = owned - owned // 16
    capacity = -(-live // peers)
    quarter = -(-capacity // shares)
    block = ceil_to(quarter + 1, 8)
    picked = peers * block
    idle_share = -(-(count - live) // shares)
    idle = ceil_to(idle_share, 16)
    own = picked + idle
    chosen = slot_index >= 0
    owner = jnp.where(chosen, slot_index // owned, peers)
    lanes = jnp.arange(peers, dtype=jnp.int32)
    match = (owner[:, None] == lanes[None, :]).astype(jnp.int32)
    rank = jnp.sum(jnp.cumsum(match, axis=0) * match, axis=1) - 1
    idle_rank = jnp.cumsum(jnp.where(chosen, 0, 1)) - 1
    piece = rank // quarter
    offset = rank % quarter
    mine = chosen & (piece % 2 == half_bit)
    far = piece // 2 ^ pair_bit
    send_row = jnp.where(mine, (owner * 2 + far) * block + offset, -1)
    picked_row = jnp.where(mine & (far == 0), owner * block + offset, -1)
    own_row = jnp.where(
        chosen,
        picked_row,
        jnp.where(idle_rank // idle_share == part, picked + idle_rank % idle_share, -1),
    )
    back_picked = jnp.where(chosen, piece * picked + owner * block + offset, -1)
    back_idle = jnp.where(chosen, -1, idle_rank // idle_share * idle + idle_rank % idle_share)
    up_all = lax.all_gather(up_weight, "tp")
    down_all = lax.all_gather(down_weight, "tp")
    send_hot = hot(jnp.arange(2 * picked, dtype=jnp.int32), send_row)
    own_hot = hot(jnp.arange(own, dtype=jnp.int32), own_row)
    send_in = mul(send_hot, tokens)
    send_hat, _ = normal_parts(send_in)
    send_rows = (send_hat * first_norm[0] + first_norm[1]).astype(BF)
    local_slot = jnp.where(chosen, slot_index % owned, 0)
    marks = jnp.stack([local_slot // 64 + 1, local_slot % 64, segment])
    block_of = jnp.where(mine, owner * 2 + far, -1)
    block_hot = jnp.arange(2 * peers, dtype=jnp.int32)[:, None] == block_of[None, :]
    mark_left = jnp.where(block_hot[None], marks[:, None, :], 0).astype(BF)
    mark_right = hot(offset, jnp.arange(128, dtype=jnp.int32))
    mark_rows = mul(mark_left.reshape(6 * peers, count), mark_right).astype(BF)
    mark_rows = mark_rows.reshape(3, 2 * peers, 128).transpose(1, 0, 2).reshape(2 * peers, 1, 384)
    mark_rows = jnp.pad(mark_rows, ((0, 0), (0, 0), (0, width - 384)))
    row_kind = jnp.arange(block, dtype=jnp.int32)[None, :, None] == quarter
    send_rows = jnp.where(row_kind, mark_rows, send_rows.reshape(2 * peers, block, width))
    got_near = lax.all_to_all(
        send_rows.reshape(peers, 2, block, width), "tok", split_axis=0, concat_axis=0, tiled=True
    )
    got_far = lax.ppermute(got_near, "tp", half_swap)
    got = jnp.stack([got_near, got_far])
    mark = got[:, :, :, quarter, :].astype(jnp.int32)
    recv_slot = (mark[..., 0:block] - 1) * 64 + mark[..., 128 : 128 + block]
    recv_segment = mark[..., 256 : 256 + block]
    slot_rows = recv_slot.transpose(0, 2, 1, 3).reshape(4 * picked)
    segment_rows = recv_segment.transpose(0, 2, 1, 3).reshape(4 * picked)
    features = got.transpose(0, 2, 1, 3, 4).reshape(4 * picked, width)
    pad = 304
    ids = jnp.arange(ROWS_DEV * pad, dtype=jnp.int32)
    slot_ids = jnp.where(ids % pad < SLOTS, ids // pad * SLOTS + ids % pad, -1000)
    slot_hot = hot(slot_ids, slot_rows)
    slot_features = mul(slot_hot, features).astype(BF)
    flat_weight = qkv_weight.reshape(width, 3 * inner)
    bias_row = jnp.concatenate([qv_bias[0], jnp.zeros_like(qv_bias[0]), qv_bias[1]])
    slot_qkv = (mul(slot_features, flat_weight) + bias_row).astype(BF)
    slot_segment = (
        jnp.sum(jnp.where(slot_hot > 0, segment_rows[None, :] + 1, 0), axis=1) - 1
    ).reshape(ROWS_DEV, pad)
    allowed = (slot_segment[:, :, None] == slot_segment[:, None, :]) & (
        slot_segment[:, None, :] >= 0
    )
    grouped = slot_qkv.reshape(ROWS_DEV, pad, 3, heads_local, HD)
    query, key, value = (grouped[:, :, 0], grouped[:, :, 1], grouped[:, :, 2])
    score_scale = HD ** (-0.5)
    scores = jnp.einsum("rqhe,rkhe->rhqk", query, key, preferred_element_type=F32) * score_scale
    scores = jnp.where(allowed[:, None], scores, MASKED_SCORE)
    top = jnp.max(scores, axis=-1, keepdims=True)
    raised = jnp.exp(scores - top)
    weights = raised / jnp.sum(raised, axis=-1, keepdims=True)
    weights_low = weights.astype(BF)
    attended = jnp.einsum("rhqk,rkhe->rqhe", weights_low, value, preferred_element_type=F32)
    heads = attended.reshape(ROWS_DEV * pad, inner).astype(BF)
    heads_rows = mul_t0(slot_hot, heads).astype(BF)
    bias_full = lax.dynamic_update_slice(
        jnp.zeros((width,), F32), out_bias, (part * (width // shares),)
    )

    def share_sum(partial):
        near, far_half = (partial[: 2 * picked], partial[2 * picked :])
        got_half = lax.ppermute(far_half.astype(BF), "tp", half_swap)
        joined = near + got_half.astype(F32)
        got_pair = lax.ppermute(joined[picked:].astype(BF), "tp", pair_swap)
        return (joined[:picked] + got_pair.astype(F32)).astype(BF)

    def across(rows):
        return lax.all_to_all(
            rows.reshape(peers, block, width), "tok", split_axis=0, concat_axis=0, tiled=True
        ).reshape(picked, width)

    returned = across(share_sum(mul(heads_rows, out_weight) + bias_full))
    own_in = mul(own_hot, tokens)
    own_cot_low = mul(own_hot, cotangent).astype(BF)
    own_cot = own_cot_low.astype(F32)
    gate = jax.nn.sigmoid(jnp.dot(own_in, router, precision=EXACT))
    branch = jnp.pad(returned.astype(F32), ((0, idle), (0, 0)))
    scale = jnp.where(jnp.arange(own) < picked, gate, 0.0)
    residual = own_in + scale[:, None] * branch
    second_hat, second_inv = normal_parts(residual)
    second = (second_hat * second_norm[0] + second_norm[1]).astype(BF)
    up_cols = up_all.transpose(1, 0, 2).reshape(width, -1)
    down_rows = down_all.reshape(-1, width)
    up_bias_all = lax.all_gather(up_bias, "tp", tiled=True)
    down_bias_all = lax.all_gather(down_bias, "tp", tiled=True)
    pre = mul(second, up_cols) + up_bias_all
    below = 0.5 * (1.0 + lax.erf(pre * 2.0 ** (-0.5)))
    bell = jnp.exp(-0.5 * pre * pre) * (2.0 * jnp.pi) ** (-0.5)
    hidden = (pre * below).astype(BF)
    layer_rows = (residual + mul(hidden, down_rows) + down_bias_all).astype(BF)
    d_hidden = mul_t1(own_cot_low, down_rows)
    d_pre = (d_hidden * (below + pre * bell)).astype(BF)
    d_down = mul_t0(hidden, own_cot_low).astype(BF).reshape(shares, -1, width)
    d_up = mul_t0(second, d_pre).astype(BF)
    d_up = d_up.reshape(width, shares, -1).transpose(1, 0, 2)
    d_second = mul_t1(d_pre, up_cols)
    d_residual = own_cot + norm_back(d_second, second_hat, second_inv, second_norm[0])
    d_branch = (d_residual[:picked] * scale[:picked, None]).astype(BF)
    d_logit = jnp.sum(d_residual * branch, axis=1) * scale * (1.0 - gate)
    small = jnp.concatenate(
        [
            jnp.sum(d_pre.astype(F32), axis=0).reshape(shares, width),
            jnp.stack(
                [
                    jnp.sum(d_second * second_hat, axis=0),
                    jnp.sum(d_second, axis=0),
                    jnp.sum(own_cot, axis=0),
                    jnp.sum(d_branch.astype(F32), axis=0),
                    jnp.sum(d_logit[:, None] * own_in, axis=0),
                ]
            ),
        ]
    )
    d_up_share = lax.psum_scatter(d_up, "tp", scatter_dimension=0)
    d_down_share = lax.psum_scatter(d_down, "tp", scatter_dimension=0)
    d_up_total = lax.psum(d_up_share, "tok").astype(F32)
    d_down_total = lax.psum(d_down_share, "tok").astype(F32)
    grad_own = across(d_branch)
    grad_near = jnp.concatenate([grad_own, lax.ppermute(grad_own, "tp", pair_swap)])
    grad_rows = jnp.concatenate([grad_near, lax.ppermute(grad_near, "tp", half_swap)])
    d_out_weight = mul_t0(heads_rows, grad_rows)
    d_heads_rows = mul_t1(grad_rows, out_weight).astype(BF)
    d_heads = mul(slot_hot, d_heads_rows).astype(BF).reshape(ROWS_DEV, pad, heads_local, HD)
    d_weights = jnp.einsum("rqhe,rkhe->rhqk", d_heads, value, preferred_element_type=F32)
    d_value = jnp.einsum("rhqk,rqhe->rkhe", weights_low, d_heads, preferred_element_type=F32)
    d_scores = (
        weights * (d_weights - jnp.sum(weights * d_weights, axis=-1, keepdims=True))
    ).astype(BF)
    d_query = jnp.einsum("rhqk,rkhe->rqhe", d_scores, key, preferred_element_type=F32) * score_scale
    d_key = jnp.einsum("rhqk,rqhe->rkhe", d_scores, query, preferred_element_type=F32) * score_scale
    d_qkv = (
        jnp.stack([d_query, d_key, d_value], axis=2).astype(BF).reshape(ROWS_DEV * pad, 3 * inner)
    )
    d_qkv_weight = mul_t0(slot_features, d_qkv)
    d_qkv_bias = jnp.sum(d_qkv.astype(F32), axis=0).reshape(3, inner)
    d_qv_bias = jnp.stack([d_qkv_bias[0], d_qkv_bias[2]])
    d_qkv_rows = mul_t0(slot_hot, d_qkv).astype(BF)
    d_normed = across(share_sum(mul_t1(d_qkv_rows, flat_weight))).astype(F32)
    d_qkv_total = lax.psum(d_qkv_weight.astype(BF), "tok").astype(F32)
    d_out_total = lax.psum(d_out_weight.astype(BF), "tok").astype(F32)
    first_hat, first_inv = normal_parts(own_in[:picked])
    d_picked = (
        d_residual[:picked]
        + norm_back(d_normed, first_hat, first_inv, first_norm[0])
        + d_logit[:picked, None] * router[None, :]
    ).astype(BF)
    d_idle = d_residual[picked:].astype(BF)

    def to_columns(rows):
        pieces = rows.reshape(rows.shape[0], shares, width // shares).transpose(1, 0, 2)
        return lax.all_to_all(pieces, "tp", split_axis=0, concat_axis=0, tiled=True).reshape(
            shares * rows.shape[0], width // shares
        )

    picked_hot = hot(back_picked, jnp.arange(shares * picked, dtype=jnp.int32))
    idle_hot = hot(back_idle, jnp.arange(shares * idle, dtype=jnp.int32))
    layer_out = (
        mul(picked_hot, to_columns(layer_rows[:picked]))
        + mul(idle_hot, to_columns(layer_rows[picked:]))
    ).astype(BF)
    d_tokens = mul(picked_hot, to_columns(d_picked)) + mul(idle_hot, to_columns(d_idle))
    first_pair = jnp.stack([jnp.sum(d_normed * first_hat, axis=0), jnp.sum(d_normed, axis=0)])
    small = lax.psum(jnp.concatenate([small, first_pair]), ("tok", "tp"))
    small_cols = columns_of(small[shares:], part, shares)
    d_up_bias = lax.dynamic_slice_in_dim(small, part, 1, 0).reshape(width)
    d_qv_bias = lax.psum(d_qv_bias, "tok")
    return (
        layer_out,
        d_tokens,
        d_qkv_total.reshape(width, 3, inner),
        d_qv_bias,
        d_out_total,
        small_cols[3],
        d_up_total,
        d_up_bias,
        d_down_total,
        small_cols[2],
        small_cols[5:7],
        small_cols[0:2],
        small_cols[4],
    )


def solution(mesh):
    return jax.shard_map(
        body,
        mesh=mesh,
        in_specs=(
            P("tok", None),
            P("tok"),
            P("tok"),
            P(),
            P(),
            P(None, None, "tp"),
            P(None, "tp"),
            P("tp", None),
            P("tp"),
            P(),
            P(None, "tp"),
            P("tp"),
            P("tp", None),
            P("tp"),
            P("tok", None),
        ),
        out_specs=(
            P("tok", "tp"),
            P("tok", "tp"),
            P(None, None, "tp"),
            P(None, "tp"),
            P("tp", None),
            P("tp"),
            P(None, "tp"),
            P("tp"),
            P("tp", None),
            P("tp"),
            P(None, "tp"),
            P(None, "tp"),
            P("tp"),
        ),
        check_vma=False,
    )
```

profile of v0, /device:TPU:0, one launch (start us, length us, event | category | flops | bytes accessed | tf_op | source)
XLA Modules:
  0.0 696.7 jit_solution(4545855774942127467)
XLA Ops:
  16.0 14.7 %fusion.135 = (f32[1152]{0:T(1024)S(1)}, f32[1152,768]{1,0:T(8,128)S(1)}) fusion(bf16[4616,768]{1,0:T(8,128)(2,1)} %param.15, s32[4616]{0:T(1024)S(1)} %get-tuple-element.46), kind=kOutput, calls=%fused_computation.269 | convolution fusion | flops 8174084096 | bytes 10652192 | tf_op jit(solution)/shard_map/dot_general | solution.py:37
  32.1 48.4 %all_to_all.40 = bf16[8,2,72,768]{3,2,1,0:T(8,128)(2,1)S(1)} all-to-all(bf16[8,2,72,768]{3,2,1,0:T(8,128)(2,1)S(1)} %broadcast_select_fusion), channel_id=1, replica_groups=mesh['tok'=8,'tp'=4] {'tok'}, dimensions={0} | all-to-all | bytes 3538944 | tf_op jit(solution)/shard_map/all_to_all | solution.py:130
  89.7 12.9 %fusion.44 = bf16[2432,768]{1,0:T(8,128)(2,1)} fusion(bf16[2304,768]{1,0:T(8,128)(2,1)} %bitcast.217, s32[2304]{0:T(1024)S(1)} %eq.201, s32[2432]{0:T(1024)S(1)} %fusion.120), kind=kOutput, calls=%fused_computation.64 | convolution fusion | flops 8614182912 | bytes 7293440 | tf_op jit(solution)/shard_map/dot_general | solution.py:37
  106.5 6.2 add_convert_fusion
  112.7 7.5 %reshape.344 = bf16[8,304,3,3,64]{1,0,4,3,2:T(8,128)(2,1)} reshape(bf16[2432,576]{0,1:T(8,128)(2,1)} %add_convert_fusion) | data formatting | bytes 5603328 | tf_op jit(solution)/shard_map/reshape | solution.py:155
  125.7 8.3 %fusion.136 = (f32[8,3,304]{2,1,0:T(4,128)S(1)}, f32[8,3,304,304]{2,3,1,0:T(8,128)}) fusion(pred[8,304,304]{1,2,0:T(8,128)(4,1)} %compare_and_fusion, bf16[8,304,1,3,64]{1,0,4,3,2:T(8,128)(2,1)S(1)} %get-tuple-element.38, bf16[8,304,1,3,64]{1,0,4,3,2:T(8,128)(2,1)S(1)} %get-tuple-element.37), kind=kOutput, calls=%fused_computation.270 | convolution fusion | flops 292774176 | bytes 11508224 | tf_op jit(solution)/shard_map/sub | solution.py:161
  158.5 15.1 %fusion.16 = f32[1200,768]{1,0:T(8,128)S(1)} fusion(bf16[4616,768]{1,0:T(8,128)(2,1)} %param.15, s32[4616]{0:T(1024)S(1)} %get-tuple-element.47), kind=kOutput, calls=%fused_computation.20 | convolution fusion | flops 8513750528 | bytes 10795040 | tf_op jit(solution)/shard_map/dot_general | solution.py:37
  178.8 20.2 %all-gather.2 = f32[4,1,768]{2,1,0:T(1,128)S(1)} all-gather(f32[1,1,768]{2,1,0:T(1,128)S(1)} %reshape.375), channel_id=1, replica_groups=mesh['tok'=8,'tp'=4] {'tp'}, dimensions={0}, use_global_device_ids=true | all-gather | bytes 15360 | tf_op jit(solution)/shard_map/all_gather | solution.py:195
  203.8 14.8 %fusion.65 = bf16[1200,768]{1,0:T(8,128)(2,1)} fusion(bf16[4616,768]{1,0:T(8,128)(2,1)} %param.29, s32[4616]{0:T(1024)S(1)} %get-tuple-element.47), kind=kOutput, calls=%fused_computation.100 | convolution fusion | flops 8514672128 | bytes 8951840 | tf_op jit(solution)/shard_map/dot_general | solution.py:37
  218.6 6.6 copy.121
  231.2 10.5 %multiply_convert_fusion = (bf16[1200,3072]{1,0:T(8,128)(2,1)S(1)}, f32[1200,3072]{1,0:T(8,128)}) fusion(f32[3072]{0:T(1024)S(1)} %bitcast.228, bf16[768,3072]{0,1:T(8,128)(2,1)S(1)} %bitcast.209, f32[768]{0:T(1024)S(1)} %get-tuple-element.24, f32[768]{0:T(1024)S(1)} %get-tuple-element.23, f32[1200]{0:T(1024)S(1)} %add_rsqrt_fusion, ...), kind=kOutput, calls=%fused_computation.34 | convolution fusion | flops 5691801600 | bytes 31440960 | tf_op jit(solution)/shard_map/dot_general | solution.py:37
  241.7 8.3 %convolution_convert_fusion = bf16[3072,768]{1,0:T(8,128)(2,1)} fusion(bf16[1200,3072]{1,0:T(8,128)(2,1)S(1)} %get-tuple-element.67, bf16[1200,768]{1,0:T(8,128)(2,1)S(1)} %copy-done.16), kind=kOutput, calls=%fused_computation.65 | convolution fusion | flops 5664669696 | bytes 13934592 | tf_op jit(solution)/shard_map/dot_general | solution.py:41
  250.2 14.4 %convert_reduce_fusion = (f32[3072]{0:T(1024)}, bf16[1200,3072]{1,0:T(8,128)(2,1)S(1)}) fusion(f32[1200,3072]{1,0:T(8,128)} %get-tuple-element.68, bf16[1200,768]{1,0:T(8,128)(2,1)} %fusion.65, bf16[3072,768]{1,0:T(8,128)(2,1)} %all-gather.8.cloned.1.call-done), kind=kOutput, calls=%fused_computation.33 | convolution fusion | flops 5706544128 | bytes 28692480 | tf_op jit(solution)/shard_map/dot_general | solution.py:45
  264.6 13.4 %multiply_reduce_fusion.2 = (f32[768]{0:T(1024)}, f32[1200]{0:T(1024)S(1)}, f32[1200]{0:T(1024)S(1)}, f32[768]{0:T(1024)}, f32[1200,768]{1,0:T(8,128)S(1)}) fusion(f32[1200]{0:T(1024)S(1)} %add_rsqrt_fusion, f32[1200]{0:T(1024)S(1)} %broadcast_multiply_fusion.2, f32[1200,768]{1,0:T(8,128)S(1)} %copy-done.3, bf16[576,768]{1,0:T(8,128)(2,1)S(1)} %bitcast.199, ...), kind=kOutput, calls=%fused_computation.86 | convolution fusion | flops 5673365504 | bytes 20382144 | tf_op jit(solution)/shard_map/dot_general | solution.py:45
  284.8 27.2 %all_to_all.41 = bf16[8,72,768]{2,1,0:T(8,128)(2,1)S(1)} all-to-all(bf16[8,72,768]{2,1,0:T(8,128)(2,1)S(1)} %bitcast.218), channel_id=1, replica_groups=mesh['tok'=8,'tp'=4] {'tok'}, dimensions={0} | all-to-all | bytes 1769472 | tf_op jit(solution)/shard_map/all_to_all | solution.py:179
  317.4 17.7 %all-reduce.4 = f32[768]{0:T(1024)} all-reduce(f32[768]{0:T(1024)} %dynamic-update-slice), channel_id=1, replica_groups=mesh['tok'=8,'tp'=4] {'tp'}, use_global_device_ids=true, to_apply=%add.4 | all-reduce | flops 768 | bytes 6144
  336.6 10.9 %convolution_convert_fusion.1 = bf16[768,3072]{1,0:T(8,128)(2,1)S(1)} fusion(bf16[1200,3072]{1,0:T(8,128)(2,1)} %copy-done.52, f32[768]{0:T(1024)} %copy-done.45, f32[768]{0:T(1024)} %copy-done.34, f32[1200]{0:T(1024)} %copy-done.31, f32[1200]{0:T(1024)S(1)} %broadcast_multiply_fusion.2, f32[1200,768]{1,0:T(8,128)} %copy-done.1, ...), kind=kOutput, calls=%fused_computation.66 | convolution fusion | flops 5672042496 | bytes 16683072 | tf_op jit(solution)/shard_map/dot_general | solution.py:41
  350.0 7.7 %fusion.56 = bf16[2432,192]{0,1:T(8,128)(2,1)} fusion(s32[2304]{0:T(1024)} %copy-done.39, s32[2432]{0:T(1024)} %copy-done.41, bf16[192,768]{1,0:T(8,128)(2,1)} %param.22, bf16[1152,768]{1,0:T(8,128)(2,1)} %collective-permute-done.4, bf16[576,768]{1,0:T(8,128)(2,1)S(1)} %collective-permute-done.3, bf16[576,768]{1,0:T(8,128)(2,1)S(1)} %bitcast.214), kind=kOutput, calls=%fused_computation.81 | convolution fusion | flops 2848284672 | bytes 4786688 | tf_op jit(solution)/shard_map/dot_general | solution.py:37
  360.5 6.4 fusion.75
  366.8 8.9 %multiply_reduce_fusion = (f32[8,3,304]{2,1,0:T(4,128)S(1)}, f32[8,3,304,304]{2,3,1,0:T(8,128)}) fusion(f32[8,3,304,304]{2,3,1,0:T(8,128)} %get-tuple-element.66, f32[8,3,304]{2,1,0:T(4,128)S(1)} %copy-done.29, bf16[8,304,1,3,64]{1,0,4,3,2:T(8,128)(2,1)S(1)} %copy-done.18, bf16[8,304,3,64]{1,0,3,2:T(8,128)(2,1)S(1)} %reshape.354), kind=kOutput, calls=%fused_computation.40 | convolution fusion | flops 290548608 | bytes 19670016 | tf_op jit(solution)/shard_map/rqhe,rkhe->rhqk/dot_general | solution.py:235
  390.2 6.7 convert_element_type.200
  396.9 16.6 %fusion.62 = f32[2304,768]{1,0:T(8,128)} fusion(bf16[768,576]{0,1:T(8,128)(2,1)S(1)} %bitcast.192, bf16[2432,576]{0,1:T(8,128)(2,1)} %convert_element_type.200, s32[2304]{0:T(1024)S(1)} %copy-done.40, s32[2432]{0:T(1024)S(1)} %copy-done.42), kind=kOutput, calls=%fused_computation.98 | convolution fusion | flops 8500396032 | bytes 10783232 | tf_op jit(solution)/shard_map/dot_general | solution.py:45
  417.8 10.6 %fusion.64 = bf16[1200,768]{1,0:T(8,128)(2,1)S(1)} fusion(bf16[1200,3072]{1,0:T(8,128)(2,1)} %copy-done.54, bf16[3072,768]{1,0:T(8,128)(2,1)} %all-gather.8.cloned.1.call-done, f32[768]{0:T(1024)S(1)} %copy-done.49, f32[1200,768]{1,0:T(8,128)} %copy-done.1, bf16[576,768]{1,0:T(8,128)(2,1)S(1)} %bitcast.202, f32[1200]{0:T(1024)S(1)} %fusion.123), kind=kOutput, calls=%fused_computation.99 | convolution fusion | flops 5667840000 | bytes 18513600 | tf_op jit(solution)/shard_map/dot_general | solution.py:37
  437.6 10.7 %all-to-all-done.2 = bf16[4,576,192]{1,2,0:T(8,128)(2,1)S(1)} async-done(((bf16[4,576,192]{1,2,0:T(8,128)(2,1)}), bf16[4,576,192]{1,2,0:T(8,128)(2,1)S(1)}, u32[]{:S(2)}, u32[]{:S(2)}) %all-to-all-start.2) | async-done | bytes 884768 | tf_op jit(solution)/shard_map/all_to_all | solution.py:262
  483.0 13.4 %fusion.2 = f32[4616,192]{0,1:T(8,128)} fusion(bf16[2496,192]{0,1:T(8,128)(2,1)} %reshape.351, s32[4616]{0:T(1024)S(1)} %copy-done.33), kind=kOutput, calls=%fused_computation.3 | convolution fusion | flops 4435791360 | bytes 4522016 | tf_op jit(solution)/shard_map/dot_general | solution.py:37
  496.5 6.8 collective-permute-done.6
  510.6 13.9 %fusion.40 = bf16[4616,192]{0,1:T(8,128)(2,1)} fusion(f32[4616,192]{0,1:T(8,128)} %fusion.2, bf16[2304,192]{0,1:T(8,128)(2,1)} %reshape.349, s32[4616]{0:T(1024)S(1)} %copy-done.32), kind=kOutput, calls=%fused_computation.57 | convolution fusion | flops 4096349184 | bytes 6220832 | tf_op jit(solution)/shard_map/dot_general | solution.py:37
  547.0 13.5 %fusion.1 = f32[4616,192]{0,1:T(8,128)} fusion(bf16[2496,192]{0,1:T(8,128)(2,1)} %reshape.359, s32[4616]{0:T(1024)S(1)} %copy-done.33), kind=kOutput, calls=%fused_computation.2 | convolution fusion | flops 4435791360 | bytes 4522016 | tf_op jit(solution)/shard_map/dot_general | solution.py:37
  560.7 23.7 %psum.43 = f32[2,192]{1,0:T(2,128)} all-reduce(f32[2,192]{1,0:T(2,128)S(1)} %pad_maximum_fusion.8), channel_id=1, replica_groups=mesh['tok'=8,'tp'=4] {'tok'}, use_global_device_ids=true, to_apply=%region_22.23 | all-reduce | flops 384 | bytes 3072 | tf_op jit(solution)/shard_map/psum | solution.py:277
  584.4 38.3 %psum.45 = f32[11,768]{1,0:T(8,128)S(1)} all-reduce(f32[11,768]{1,0:T(8,128)S(1)} %concatenate.16), channel_id=1, replica_groups=mesh['tok'=8,'tp'=4] {'tok','tp'}, use_global_device_ids=true, to_apply=%region_32.33 | all-reduce | flops 8448 | bytes 67584 | tf_op jit(solution)/shard_map/psum | solution.py:274
  626.1 13.6 %fusion.39 = f32[4616,192]{0,1:T(8,128)} fusion(f32[4616,192]{0,1:T(8,128)} %fusion.1, bf16[2304,192]{0,1:T(8,128)(2,1)S(1)} %reshape.357, s32[4616]{0:T(1024)S(1)} %copy-done.32), kind=kOutput, calls=%fused_computation.56 | convolution fusion | flops 4095462912 | bytes 7993376 | tf_op jit(solution)/shard_map/dot_general | solution.py:37
  639.7 42.5 %all-reduce.8.cloned.1.call-done = (bf16[768,3,192]{0,2,1:T(8,128)(2,1)}, bf16[192,768]{1,0:T(8,128)(2,1)}, bf16[768,768]{1,0:T(8,128)(2,1)}, bf16[768,768]{1,0:T(8,128)(2,1)}) async-done(((bf16[768,3,192]{0,2,1:T(8,128)(2,1)}, bf16[192,768]{1,0:T(8,128)(2,1)}, bf16[768,768]{1,0:T(8,128)(2,1)}, bf16[768,768]{1,0:T(8,128)(2,1)}), (bf16[768,3,192]{0,2,1:T(8,128)(2,1)}, bf16[192,768]{1,0:T(8,128)(2,1)}, ...) | async-done | bytes 3538960 | tf_op jit(solution)/shard_map/psum | solution.py:250
  (301 shorter events, 190.2 us)
Async XLA Ops:
  7.2 99.3 %copy-start = (bf16[768,3,192]{0,2,1:T(8,128)(2,1)S(1)}, bf16[768,3,192]{0,2,1:T(8,128)(2,1)}, u32[]{:S(2)}) copy-start(bf16[768,3,192]{0,2,1:T(8,128)(2,1)} %param.20) | copy-start | bytes 2654212
  7.2 211.4 %all-gather.6.cloned.1.call-start = ((), (), s32[]{:S(2)}) async-start(), calls=%async_computation.12 | async-start | bytes 5898240 | tf_op jit(solution)/shard_map/all_gather | solution.py:112
  8.1 23.2 %copy-start.23 = (f32[768]{0:T(1024)}, f32[768]{0:T(1024)S(1)}, u32[]{:S(2)}) copy-start(f32[768]{0:T(1024)S(1)} %get-tuple-element.21) | copy-start | bytes 9220
  32.1 49.1 %copy-start.51 = (f32[192]{0:T(256)S(1)}, f32[192]{0:T(256)}, u32[]{:S(2)}) copy-start(f32[192]{0:T(256)} %param.23) | copy-start | bytes 2308
  32.1 49.4 %copy-start.50 = (f32[2,192]{1,0:T(2,128)S(1)}, f32[2,192]{1,0:T(2,128)}, u32[]{:S(2)}) copy-start(f32[2,192]{1,0:T(2,128)} %param.21) | copy-start | bytes 4612
  80.6 3.9 collective-permute-start
  80.7 169.5 %all-gather.8.cloned.1.call-start = ((), (), s32[]{:S(2)}) async-start(), calls=%async_computation.13 | async-start | bytes 5898240 | tf_op jit(solution)/shard_map/all_gather | solution.py:113
  81.6 59.8 %copy-start.41 = (s32[2432]{0:T(1024)}, s32[2432]{0:T(1024)S(1)}, u32[]{:S(2)}) copy-start(s32[2432]{0:T(1024)S(1)} %fusion.120) | copy-start | bytes 29188
  89.7 51.7 %copy-start.39 = (s32[2304]{0:T(1024)}, s32[2304]{0:T(1024)S(1)}, u32[]{:S(2)}) copy-start(s32[2304]{0:T(1024)S(1)} %eq.201) | copy-start | bytes 27652
  149.8 3.9 collective-permute-start.1
  157.1 42.0 %collective-permute-start.2 = (bf16[576,768]{1,0:T(8,128)(2,1)S(1)}, bf16[576,768]{1,0:T(8,128)(2,1)S(1)}, u32[]{:S(2)}, u32[]{:S(2)}) collective-permute-start(bf16[576,768]{1,0:T(8,128)(2,1)S(1)} %slice.292), channel_id=1, source_target_pairs={{0,2},{1,3},{2,0},{3,1},{4,6},{5,7},{6,4},{7,5},{8,10},{9,11},{10,... | collective-permute-start | bytes 2654216 | tf_op jit(solution)/shard_map/ppermute | solution.py:175
  173.6 25.4 %copy-start.44 = (f32[2,768]{1,0:T(2,128)S(1)}, f32[2,768]{1,0:T(2,128)}, u32[]{:S(2)}) copy-start(f32[2,768]{1,0:T(2,128)} %param.24) | copy-start | bytes 18436
  178.8 21.4 %copy-start.25 = (f32[1200]{0:T(1024)}, f32[1200]{0:T(1024)S(1)}, u32[]{:S(2)}) copy-start(f32[1200]{0:T(1024)S(1)} %convolution_reduce_fusion) | copy-start | bytes 14404
  199.0 31.7 %copy-start.45 = (f32[768]{0:T(1024)}, f32[768]{0:T(1024)S(1)}, u32[]{:S(2)}) copy-start(f32[768]{0:T(1024)S(1)} %get-tuple-element.24) | copy-start | bytes 9220
  199.1 78.9 %copy-start.34 = (f32[768]{0:T(1024)}, f32[768]{0:T(1024)S(1)}, u32[]{:S(2)}) copy-start(f32[768]{0:T(1024)S(1)} %get-tuple-element.23) | copy-start | bytes 9220
  200.2 26.5 %all-to-all-start.1 = ((bf16[8,72,768]{2,1,0:T(8,128)(2,1)}), bf16[8,72,768]{2,1,0:T(8,128)(2,1)S(1)}, u32[]{:S(2)}, u32[]{:S(2)}) async-start(bf16[8,72,768]{2,1,0:T(8,128)(2,1)} %bitcast.21), calls=%async_computation.1 | async-start | bytes 1769472 | tf_op jit(solution)/shard_map/all_to_all | solution.py:179
  203.7 335.6 %reduce-scatter.5.cloned.1.call-start = ((), (), s32[]{:S(2)}) async-start(), calls=%async_computation.11 | async-start | bytes 5898240 | tf_op jit(solution)/shard_map/reduce_scatter | solution.py:226
  230.8 47.2 %copy-start.31 = (f32[1200]{0:T(1024)}, f32[1200]{0:T(1024)S(1)}, u32[]{:S(2)}) copy-start(f32[1200]{0:T(1024)S(1)} %add_rsqrt_fusion) | copy-start | bytes 14404
  250.1 289.3 %reduce-scatter.3.cloned.1.call-start = ((), (), s32[]{:S(2)}) async-start(), calls=%async_computation.10 | async-start | bytes 5898240 | tf_op jit(solution)/shard_map/reduce_scatter | solution.py:225
  312.0 38.1 %copy-start.13 = (bf16[8,72,768]{2,1,0:T(8,128)(2,1)}, bf16[8,72,768]{2,1,0:T(8,128)(2,1)S(1)}, u32[]{:S(2)}) copy-start(bf16[8,72,768]{2,1,0:T(8,128)(2,1)S(1)} %all_to_all.41) | copy-start | bytes 2654212
  312.0 23.2 %collective-permute-start.3 = (bf16[576,768]{1,0:T(8,128)(2,1)S(1)}, bf16[576,768]{1,0:T(8,128)(2,1)S(1)}, u32[]{:S(2)}, u32[]{:S(2)}) collective-permute-start(bf16[576,768]{1,0:T(8,128)(2,1)S(1)} %bitcast.212), channel_id=1, source_target_pairs={{0,2},{1,3},{2,0},{3,1},{4,6},{5,7},{6,4},{7,5},{8,10},{9,11},{10,... | collective-permute-start | bytes 2654216 | tf_op jit(solution)/shard_map/ppermute | solution.py:230
  336.6 13.4 %collective-permute-start.4 = (bf16[1152,768]{1,0:T(8,128)(2,1)}, bf16[1152,768]{1,0:T(8,128)(2,1)}, u32[]{:S(2)}, u32[]{:S(2)}) collective-permute-start(bf16[1152,768]{1,0:T(8,128)(2,1)} %pad_maximum_fusion.2), channel_id=1, source_target_pairs={{0,1},{1,0},{2,3},{3,2},{4,5},{5,4},{6,7},{7,6},{8,9},{9,8},{10,11... | collective-permute-start | bytes 5308424 | tf_op jit(solution)/shard_map/ppermute | solution.py:231
  396.9 20.9 %copy-start.49 = (f32[768]{0:T(1024)S(1)}, f32[768]{0:T(1024)}, u32[]{:S(2)}) copy-start(f32[768]{0:T(1024)} %all-reduce.4) | copy-start | bytes 9220
  417.3 58.1 %collective-permute-start.5 = (bf16[1152,768]{1,0:T(8,128)(2,1)}, bf16[1152,768]{1,0:T(8,128)(2,1)}, u32[]{:S(2)}, u32[]{:S(2)}) collective-permute-start(bf16[1152,768]{1,0:T(8,128)(2,1)} %slice.288), channel_id=1, source_target_pairs={{0,1},{1,0},{2,3},{3,2},{4,5},{5,4},{6,7},{7,6},{8,9},{9,8},{10,11... | collective-permute-start | bytes 5308424 | tf_op jit(solution)/shard_map/ppermute | solution.py:173
  431.0 17.2 %all-to-all-start.2 = ((bf16[4,576,192]{1,2,0:T(8,128)(2,1)}), bf16[4,576,192]{1,2,0:T(8,128)(2,1)S(1)}, u32[]{:S(2)}, u32[]{:S(2)}) async-start(bf16[4,576,192]{1,2,0:T(8,128)(2,1)} %bitcast.29), calls=%async_computation.2 | async-start | bytes 1966080 | tf_op jit(solution)/shard_map/all_to_all | solution.py:262
  436.2 19.8 %copy-start.26 = (f32[1200]{0:T(1024)S(1)}, f32[1200]{0:T(1024)}, u32[]{:S(2)}) copy-start(f32[1200]{0:T(1024)} %copy-done.25) | copy-start | bytes 14404
  448.2 18.1 %all-to-all-start.3 = ((bf16[4,624,192]{1,2,0:T(8,128)(2,1)}), bf16[4,624,192]{1,2,0:T(8,128)(2,1)}, u32[]{:S(2)}, u32[]{:S(2)}) async-start(bf16[4,624,192]{1,2,0:T(8,128)(2,1)} %bitcast.31), calls=%async_computation.3 | async-start | bytes 1966080 | tf_op jit(solution)/shard_map/all_to_all | solution.py:262
  466.3 39.6 %all-to-all-start.7 = ((bf16[4,624,192]{1,2,0:T(8,128)(2,1)}), bf16[4,624,192]{1,2,0:T(8,128)(2,1)S(1)}, u32[]{:S(2)}, u32[]{:S(2)}) async-start(bf16[4,624,192]{1,2,0:T(8,128)(2,1)} %bitcast.211), calls=%async_computation.7 | async-start | bytes 1966080 | tf_op jit(solution)/shard_map/all_to_all | solution.py:262
  481.1 22.2 %collective-permute-start.6 = (bf16[576,768]{1,0:T(8,128)(2,1)}, bf16[576,768]{1,0:T(8,128)(2,1)S(1)}, u32[]{:S(2)}, u32[]{:S(2)}) collective-permute-start(bf16[576,768]{1,0:T(8,128)(2,1)} %slice.291), channel_id=1, source_target_pairs={{0,2},{1,3},{2,0},{3,1},{4,6},{5,7},{6,4},{7,5},{8,10},{9,11},{10,... | collective-permute-start | bytes 2654216 | tf_op jit(solution)/shard_map/ppermute | solution.py:175
  505.9 30.6 %all-to-all-start.5 = ((bf16[8,72,768]{2,1,0:T(8,128)(2,1)}), bf16[8,72,768]{2,1,0:T(8,128)(2,1)S(1)}, u32[]{:S(2)}, u32[]{:S(2)}) async-start(bf16[8,72,768]{2,1,0:T(8,128)(2,1)} %bitcast.216), calls=%async_computation.5 | async-start | bytes 1769472 | tf_op jit(solution)/shard_map/all_to_all | solution.py:179
  510.6 171.6 %all-reduce.8.cloned.1.call-start = ((), (), s32[]{:S(2)}) async-start(), calls=%async_computation.14 | async-start | bytes 7077888 | tf_op jit(solution)/shard_map/psum | solution.py:250
  543.3 81.4 %all-to-all-start.6 = ((bf16[4,576,192]{1,2,0:T(8,128)(2,1)}), bf16[4,576,192]{1,2,0:T(8,128)(2,1)S(1)}, u32[]{:S(2)}, u32[]{:S(2)}) async-start(bf16[4,576,192]{1,2,0:T(8,128)(2,1)} %bitcast.43), calls=%async_computation.6 | async-start | bytes 1966080 | tf_op jit(solution)/shard_map/all_to_all | solution.py:262
  (46 other events, 388.6 us)
Sparse Core Ops, SparseCore 0:
  80.8 36.5 all-gather.5
  150.1 55.4 all-gather.7
  250.2 47.7 reduce-scatter.4
  350.1 46.8 reduce-scatter.2
  539.5 142.6 all-reduce.7
where the time goes:
time: 705 us; the launch traced here: 697 us
  matrix products  260 us (37%)
  blocking collectives  175 us (25%)
  local copies, waits for them, and re-layouts  80 us (11%)
  waiting for transfers between devices  72.2 us (10%)
  other arithmetic  63.8 us (9%)
  starting transfers between devices  29.5 us (4%)
  between operations  16.1 us (2%)
    dot_general x14, matrix products, mul(): lax.dot_general(left, right, (((1,), (0,)), ((), ())), preferred_element_...  149 us
    all_to_all x1, blocking collectives, body(): lax.all_to_all(send_rows.reshape(peers, 2, block, width), 'tok', split_ax...  48.4 us
    dot_general x3, matrix products, mul_t1(): lax.dot_general(left, right, (((1,), (1,)), ((), ())), preferred_element_...  44.5 us
    psum x1, waiting for transfers between devices, body(): d_qkv_total = lax.psum(d_qkv_weight.astype(BF), 'tok').astype(F32)  42.5 us
    psum x1, blocking collectives, body(): small = lax.psum(jnp.concatenate([small, first_pair]), ('tok', 'tp'))  38.3 us
    dot_general x5, matrix products, mul_t0(): lax.dot_general(left, right, (((0,), (0,)), ((), ())), preferred_element_...  30.6 us
    all_to_all x1, blocking collectives, across(): lax.all_to_all(rows.reshape(peers, block, width), 'tok', split_axis=0, co...  27.2 us
    psum x1, blocking collectives, body(): d_qv_bias = lax.psum(d_qv_bias, 'tok')  23.7 us
  transfers between devices with their start and end apart: 18, of which 7 were waited for; matrix products, arithmetic and copies ran while one was open for 52% of the time, Pallas kernels for 0%

commit v1 on v0

--- a/solution.py
+++ b/solution.py
@@ -274,7 +274,7 @@
     small = lax.psum(jnp.concatenate([small, first_pair]), ("tok", "tp"))
     small_cols = columns_of(small[shares:], part, shares)
     d_up_bias = lax.dynamic_slice_in_dim(small, part, 1, 0).reshape(width)
-    d_qv_bias = lax.psum(d_qv_bias, "tok")
+    d_qv_bias = jnp.sum(lax.all_gather(d_qv_bias, "tok"), axis=0)
     return (
         layer_out,
         d_tokens,

time: 705 us -> 705 us (level)
    all_gather x0 -> x1, blocking collectives: none -> 28.6 us  [body(): d_qv_bias = jnp.sum(lax.all_gather(d_qv_bias, 'tok'), axis=0)]
    psum x1 -> x0, blocking collectives: 23.7 us -> none  [body(): d_qv_bias = lax.psum(d_qv_bias, 'tok')]
where the time goes in v1:
time: 705 us; the launch traced here: 697 us
  matrix products  260 us (37%)
  blocking collectives  182 us (26%)
  local copies, waits for them, and re-layouts  80 us (11%)
  waiting for transfers between devices  66.1 us (9%)
  other arithmetic  64.4 us (9%)
  starting transfers between devices  29.5 us (4%)
  between operations  16.1 us (2%)
    dot_general x14, matrix products, mul(): lax.dot_general(left, right, (((1,), (0,)), ((), ())), preferred_element_...  149 us
    all_to_all x1, blocking collectives, body(): lax.all_to_all(send_rows.reshape(peers, 2, block, width), 'tok', split_ax...  48.4 us
    dot_general x3, matrix products, mul_t1(): lax.dot_general(left, right, (((1,), (1,)), ((), ())), preferred_element_...  44.4 us
    psum x1, blocking collectives, body(): small = lax.psum(jnp.concatenate([small, first_pair]), ('tok', 'tp'))  39.4 us
    psum x1, waiting for transfers between devices, body(): d_qkv_total = lax.psum(d_qkv_weight.astype(BF), 'tok').astype(F32)  36.4 us
    dot_general x5, matrix products, mul_t0(): lax.dot_general(left, right, (((0,), (0,)), ((), ())), preferred_element_...  30.6 us
    all_gather x1, blocking collectives, body(): d_qv_bias = jnp.sum(lax.all_gather(d_qv_bias, 'tok'), axis=0)  28.6 us
    all_to_all x1, blocking collectives, across(): lax.all_to_all(rows.reshape(peers, block, width), 'tok', split_axis=0, co...  27.2 us
  transfers between devices with their start and end apart: 18, of which 7 were waited for; matrix products, arithmetic and copies ran while one was open for 52% of the time, Pallas kernels for 0%

profile of v1, /device:TPU:0, one launch (start us, length us, event | category | flops | bytes accessed | tf_op | source)
XLA Modules:
  0.0 697.2 jit_solution(2372863380445407270)
XLA Ops:
  16.0 14.7 %fusion.135 = (f32[1152]{0:T(1024)S(1)}, f32[1152,768]{1,0:T(8,128)S(1)}) fusion(bf16[4616,768]{1,0:T(8,128)(2,1)} %param.15, s32[4616]{0:T(1024)S(1)} %get-tuple-element.46), kind=kOutput, calls=%fused_computation.269 | convolution fusion | flops 8174084096 | bytes 10652192 | tf_op jit(solution)/shard_map/dot_general | solution.py:37
  32.1 48.4 %all_to_all.40 = bf16[8,2,72,768]{3,2,1,0:T(8,128)(2,1)S(1)} all-to-all(bf16[8,2,72,768]{3,2,1,0:T(8,128)(2,1)S(1)} %broadcast_select_fusion), channel_id=1, replica_groups=mesh['tok'=8,'tp'=4] {'tok'}, dimensions={0} | all-to-all | bytes 3538944 | tf_op jit(solution)/shard_map/all_to_all | solution.py:130
  89.7 12.9 %fusion.44 = bf16[2432,768]{1,0:T(8,128)(2,1)} fusion(bf16[2304,768]{1,0:T(8,128)(2,1)} %bitcast.219, s32[2304]{0:T(1024)S(1)} %eq.201, s32[2432]{0:T(1024)S(1)} %fusion.120), kind=kOutput, calls=%fused_computation.64 | convolution fusion | flops 8614182912 | bytes 7293440 | tf_op jit(solution)/shard_map/dot_general | solution.py:37
  106.5 6.2 add_convert_fusion
  112.7 7.5 %reshape.344 = bf16[8,304,3,3,64]{1,0,4,3,2:T(8,128)(2,1)} reshape(bf16[2432,576]{0,1:T(8,128)(2,1)} %add_convert_fusion) | data formatting | bytes 5603328 | tf_op jit(solution)/shard_map/reshape | solution.py:155
  125.7 8.3 %fusion.136 = (f32[8,3,304]{2,1,0:T(4,128)S(1)}, f32[8,3,304,304]{2,3,1,0:T(8,128)}) fusion(pred[8,304,304]{1,2,0:T(8,128)(4,1)} %compare_and_fusion, bf16[8,304,1,3,64]{1,0,4,3,2:T(8,128)(2,1)S(1)} %get-tuple-element.38, bf16[8,304,1,3,64]{1,0,4,3,2:T(8,128)(2,1)S(1)} %get-tuple-element.37), kind=kOutput, calls=%fused_computation.270 | convolution fusion | flops 292774176 | bytes 11508224 | tf_op jit(solution)/shard_map/sub | solution.py:161
  158.5 15.1 %fusion.16 = f32[1200,768]{1,0:T(8,128)S(1)} fusion(bf16[4616,768]{1,0:T(8,128)(2,1)} %param.15, s32[4616]{0:T(1024)S(1)} %get-tuple-element.47), kind=kOutput, calls=%fused_computation.20 | convolution fusion | flops 8513750528 | bytes 10795040 | tf_op jit(solution)/shard_map/dot_general | solution.py:37
  178.8 20.2 %all-gather.3 = f32[4,1,768]{2,1,0:T(1,128)S(1)} all-gather(f32[1,1,768]{2,1,0:T(1,128)S(1)} %reshape.376), channel_id=1, replica_groups=mesh['tok'=8,'tp'=4] {'tp'}, dimensions={0}, use_global_device_ids=true | all-gather | bytes 15360 | tf_op jit(solution)/shard_map/all_gather | solution.py:195
  203.8 14.8 %fusion.65 = bf16[1200,768]{1,0:T(8,128)(2,1)} fusion(bf16[4616,768]{1,0:T(8,128)(2,1)} %param.29, s32[4616]{0:T(1024)S(1)} %get-tuple-element.47), kind=kOutput, calls=%fused_computation.100 | convolution fusion | flops 8514672128 | bytes 8951840 | tf_op jit(solution)/shard_map/dot_general | solution.py:37
  218.6 6.6 copy.121
  231.2 10.5 %multiply_convert_fusion = (bf16[1200,3072]{1,0:T(8,128)(2,1)S(1)}, f32[1200,3072]{1,0:T(8,128)}) fusion(f32[3072]{0:T(1024)S(1)} %bitcast.230, bf16[768,3072]{0,1:T(8,128)(2,1)S(1)} %bitcast.211, f32[768]{0:T(1024)S(1)} %get-tuple-element.24, f32[768]{0:T(1024)S(1)} %get-tuple-element.23, f32[1200]{0:T(1024)S(1)} %add_rsqrt_fusion, ...), kind=kOutput, calls=%fused_computation.34 | convolution fusion | flops 5691801600 | bytes 31440960 | tf_op jit(solution)/shard_map/dot_general | solution.py:37
  241.7 8.3 %convolution_convert_fusion = bf16[3072,768]{1,0:T(8,128)(2,1)} fusion(bf16[1200,3072]{1,0:T(8,128)(2,1)S(1)} %get-tuple-element.67, bf16[1200,768]{1,0:T(8,128)(2,1)S(1)} %copy-done.16), kind=kOutput, calls=%fused_computation.65 | convolution fusion | flops 5664669696 | bytes 13934592 | tf_op jit(solution)/shard_map/dot_general | solution.py:41
  250.2 14.4 %convert_reduce_fusion = (f32[3072]{0:T(1024)}, bf16[1200,3072]{1,0:T(8,128)(2,1)S(1)}) fusion(f32[1200,3072]{1,0:T(8,128)} %get-tuple-element.68, bf16[1200,768]{1,0:T(8,128)(2,1)} %fusion.65, bf16[3072,768]{1,0:T(8,128)(2,1)} %all-gather.10.cloned.1.call-done), kind=kOutput, calls=%fused_computation.33 | convolution fusion | flops 5706544128 | bytes 28692480 | tf_op jit(solution)/shard_map/dot_general | solution.py:45
  264.6 13.4 %multiply_reduce_fusion.2 = (f32[768]{0:T(1024)}, f32[1200]{0:T(1024)S(1)}, f32[1200]{0:T(1024)S(1)}, f32[768]{0:T(1024)}, f32[1200,768]{1,0:T(8,128)S(1)}) fusion(f32[1200]{0:T(1024)S(1)} %add_rsqrt_fusion, f32[1200]{0:T(1024)S(1)} %broadcast_multiply_fusion.2, f32[1200,768]{1,0:T(8,128)S(1)} %copy-done.3, bf16[576,768]{1,0:T(8,128)(2,1)S(1)} %bitcast.201, ...), kind=kOutput, calls=%fused_computation.86 | convolution fusion | flops 5673365504 | bytes 20382144 | tf_op jit(solution)/shard_map/dot_general | solution.py:45
  284.8 27.2 %all_to_all.41 = bf16[8,72,768]{2,1,0:T(8,128)(2,1)S(1)} all-to-all(bf16[8,72,768]{2,1,0:T(8,128)(2,1)S(1)} %bitcast.220), channel_id=1, replica_groups=mesh['tok'=8,'tp'=4] {'tok'}, dimensions={0} | all-to-all | bytes 1769472 | tf_op jit(solution)/shard_map/all_to_all | solution.py:179
  317.4 17.8 %all-reduce.4 = f32[768]{0:T(1024)} all-reduce(f32[768]{0:T(1024)} %dynamic-update-slice), channel_id=1, replica_groups=mesh['tok'=8,'tp'=4] {'tp'}, use_global_device_ids=true, to_apply=%add.4 | all-reduce | flops 768 | bytes 6144
  336.6 10.9 %convolution_convert_fusion.1 = bf16[768,3072]{1,0:T(8,128)(2,1)S(1)} fusion(bf16[1200,3072]{1,0:T(8,128)(2,1)} %copy-done.52, f32[768]{0:T(1024)} %copy-done.45, f32[768]{0:T(1024)} %copy-done.34, f32[1200]{0:T(1024)} %copy-done.31, f32[1200]{0:T(1024)S(1)} %broadcast_multiply_fusion.2, f32[1200,768]{1,0:T(8,128)} %copy-done.1, ...), kind=kOutput, calls=%fused_computation.66 | convolution fusion | flops 5672042496 | bytes 16683072 | tf_op jit(solution)/shard_map/dot_general | solution.py:41
  350.0 7.7 %fusion.56 = bf16[2432,192]{0,1:T(8,128)(2,1)} fusion(s32[2304]{0:T(1024)} %copy-done.39, s32[2432]{0:T(1024)} %copy-done.41, bf16[192,768]{1,0:T(8,128)(2,1)} %param.22, bf16[1152,768]{1,0:T(8,128)(2,1)} %collective-permute-done.4, bf16[576,768]{1,0:T(8,128)(2,1)S(1)} %collective-permute-done.3, bf16[576,768]{1,0:T(8,128)(2,1)S(1)} %bitcast.216), kind=kOutput, calls=%fused_computation.81 | convolution fusion | flops 2848284672 | bytes 4786688 | tf_op jit(solution)/shard_map/dot_general | solution.py:37
  360.4 6.4 fusion.75
  366.8 8.9 %multiply_reduce_fusion = (f32[8,3,304]{2,1,0:T(4,128)S(1)}, f32[8,3,304,304]{2,3,1,0:T(8,128)}) fusion(f32[8,3,304,304]{2,3,1,0:T(8,128)} %get-tuple-element.66, f32[8,3,304]{2,1,0:T(4,128)S(1)} %copy-done.29, bf16[8,304,1,3,64]{1,0,4,3,2:T(8,128)(2,1)S(1)} %copy-done.18, bf16[8,304,3,64]{1,0,3,2:T(8,128)(2,1)S(1)} %reshape.354), kind=kOutput, calls=%fused_computation.40 | convolution fusion | flops 290548608 | bytes 19670016 | tf_op jit(solution)/shard_map/rqhe,rkhe->rhqk/dot_general | solution.py:235
  390.1 6.7 convert_element_type.200
  396.9 16.6 %fusion.62 = f32[2304,768]{1,0:T(8,128)} fusion(bf16[768,576]{0,1:T(8,128)(2,1)S(1)} %bitcast.194, bf16[2432,576]{0,1:T(8,128)(2,1)} %convert_element_type.200, s32[2304]{0:T(1024)S(1)} %copy-done.40, s32[2432]{0:T(1024)S(1)} %copy-done.42), kind=kOutput, calls=%fused_computation.98 | convolution fusion | flops 8500396032 | bytes 10783232 | tf_op jit(solution)/shard_map/dot_general | solution.py:45
  417.7 10.6 %fusion.64 = bf16[1200,768]{1,0:T(8,128)(2,1)S(1)} fusion(bf16[1200,3072]{1,0:T(8,128)(2,1)} %copy-done.54, bf16[3072,768]{1,0:T(8,128)(2,1)} %all-gather.10.cloned.1.call-done, f32[768]{0:T(1024)S(1)} %copy-done.49, f32[1200,768]{1,0:T(8,128)} %copy-done.1, bf16[576,768]{1,0:T(8,128)(2,1)S(1)} %bitcast.204, f32[1200]{0:T(1024)S(1)} %fusion.123), kind=kOutput, calls=%fused_computation.99 | convolution fusion | flops 5667840000 | bytes 18513600 | tf_op jit(solution)/shard_map/dot_general | solution.py:37
  437.5 10.7 %all-to-all-done.2 = bf16[4,576,192]{1,2,0:T(8,128)(2,1)S(1)} async-done(((bf16[4,576,192]{1,2,0:T(8,128)(2,1)}), bf16[4,576,192]{1,2,0:T(8,128)(2,1)S(1)}, u32[]{:S(2)}, u32[]{:S(2)}) %all-to-all-start.2) | async-done | bytes 884768 | tf_op jit(solution)/shard_map/all_to_all | solution.py:262
  483.0 13.4 %fusion.2 = f32[4616,192]{0,1:T(8,128)} fusion(bf16[2496,192]{0,1:T(8,128)(2,1)} %reshape.351, s32[4616]{0:T(1024)S(1)} %copy-done.33), kind=kOutput, calls=%fused_computation.3 | convolution fusion | flops 4435791360 | bytes 4522016 | tf_op jit(solution)/shard_map/dot_general | solution.py:37
  496.5 6.8 collective-permute-done.6
  510.7 13.9 %fusion.40 = bf16[4616,192]{0,1:T(8,128)(2,1)} fusion(f32[4616,192]{0,1:T(8,128)} %fusion.2, bf16[2304,192]{0,1:T(8,128)(2,1)} %reshape.349, s32[4616]{0:T(1024)S(1)} %copy-done.32), kind=kOutput, calls=%fused_computation.57 | convolution fusion | flops 4096349184 | bytes 6220832 | tf_op jit(solution)/shard_map/dot_general | solution.py:37
  547.1 13.5 %fusion.1 = f32[4616,192]{0,1:T(8,128)} fusion(bf16[2496,192]{0,1:T(8,128)(2,1)} %reshape.359, s32[4616]{0:T(1024)S(1)} %copy-done.33), kind=kOutput, calls=%fused_computation.2 | convolution fusion | flops 4435791360 | bytes 4522016 | tf_op jit(solution)/shard_map/dot_general | solution.py:37
  560.7 28.6 %all-gather.4 = f32[8,2,192]{2,1,0:T(2,128)S(1)} all-gather(f32[1,2,192]{2,1,0:T(2,128)S(1)} %maximum_bitcast_fusion), channel_id=4, replica_groups=mesh['tok'=8,'tp'=4] {'tok'}, dimensions={0}, use_global_device_ids=true | all-gather | bytes 13824 | tf_op jit(solution)/shard_map/all_gather | solution.py:277
  589.9 39.4 %psum.37 = f32[11,768]{1,0:T(8,128)S(1)} all-reduce(f32[11,768]{1,0:T(8,128)S(1)} %concatenate.16), channel_id=1, replica_groups=mesh['tok'=8,'tp'=4] {'tok','tp'}, use_global_device_ids=true, to_apply=%region_32.33 | all-reduce | flops 8448 | bytes 67584 | tf_op jit(solution)/shard_map/psum | solution.py:274
  632.8 13.6 %fusion.39 = f32[4616,192]{0,1:T(8,128)} fusion(f32[4616,192]{0,1:T(8,128)} %fusion.1, bf16[2304,192]{0,1:T(8,128)(2,1)S(1)} %reshape.357, s32[4616]{0:T(1024)S(1)} %copy-done.32), kind=kOutput, calls=%fused_computation.56 | convolution fusion | flops 4095462912 | bytes 7993376 | tf_op jit(solution)/shard_map/dot_general | solution.py:37
  646.3 36.4 %all-reduce.8.cloned.1.call-done = (bf16[768,3,192]{0,2,1:T(8,128)(2,1)}, bf16[192,768]{1,0:T(8,128)(2,1)}, bf16[768,768]{1,0:T(8,128)(2,1)}, bf16[768,768]{1,0:T(8,128)(2,1)}) async-done(((bf16[768,3,192]{0,2,1:T(8,128)(2,1)}, bf16[192,768]{1,0:T(8,128)(2,1)}, bf16[768,768]{1,0:T(8,128)(2,1)}, bf16[768,768]{1,0:T(8,128)(2,1)}), (bf16[768,3,192]{0,2,1:T(8,128)(2,1)}, bf16[192,768]{1,0:T(8,128)(2,1)}, ...) | async-done | bytes 3538960 | tf_op jit(solution)/shard_map/psum | solution.py:250
  (302 shorter events, 190.9 us)
Async XLA Ops:
  7.2 99.3 %copy-start = (bf16[768,3,192]{0,2,1:T(8,128)(2,1)S(1)}, bf16[768,3,192]{0,2,1:T(8,128)(2,1)}, u32[]{:S(2)}) copy-start(bf16[768,3,192]{0,2,1:T(8,128)(2,1)} %param.20) | copy-start | bytes 2654212
  7.2 211.4 %all-gather.8.cloned.1.call-start = ((), (), s32[]{:S(2)}) async-start(), calls=%async_computation.12 | async-start | bytes 5898240 | tf_op jit(solution)/shard_map/all_gather | solution.py:112
  8.1 23.2 %copy-start.23 = (f32[768]{0:T(1024)}, f32[768]{0:T(1024)S(1)}, u32[]{:S(2)}) copy-start(f32[768]{0:T(1024)S(1)} %get-tuple-element.21) | copy-start | bytes 9220
  32.1 49.1 %copy-start.51 = (f32[192]{0:T(256)S(1)}, f32[192]{0:T(256)}, u32[]{:S(2)}) copy-start(f32[192]{0:T(256)} %param.23) | copy-start | bytes 2308
  32.1 49.4 %copy-start.50 = (f32[2,192]{1,0:T(2,128)S(1)}, f32[2,192]{1,0:T(2,128)}, u32[]{:S(2)}) copy-start(f32[2,192]{1,0:T(2,128)} %param.21) | copy-start | bytes 4612
  80.6 3.9 collective-permute-start
  80.7 169.5 %all-gather.10.cloned.1.call-start = ((), (), s32[]{:S(2)}) async-start(), calls=%async_computation.13 | async-start | bytes 5898240 | tf_op jit(solution)/shard_map/all_gather | solution.py:113
  81.6 59.8 %copy-start.41 = (s32[2432]{0:T(1024)}, s32[2432]{0:T(1024)S(1)}, u32[]{:S(2)}) copy-start(s32[2432]{0:T(1024)S(1)} %fusion.120) | copy-start | bytes 29188
  89.7 51.8 %copy-start.39 = (s32[2304]{0:T(1024)}, s32[2304]{0:T(1024)S(1)}, u32[]{:S(2)}) copy-start(s32[2304]{0:T(1024)S(1)} %eq.201) | copy-start | bytes 27652
  149.8 3.9 collective-permute-start.1
  157.1 42.0 %collective-permute-start.2 = (bf16[576,768]{1,0:T(8,128)(2,1)S(1)}, bf16[576,768]{1,0:T(8,128)(2,1)S(1)}, u32[]{:S(2)}, u32[]{:S(2)}) collective-permute-start(bf16[576,768]{1,0:T(8,128)(2,1)S(1)} %slice.292), channel_id=1, source_target_pairs={{0,2},{1,3},{2,0},{3,1},{4,6},{5,7},{6,4},{7,5},{8,10},{9,11},{10,... | collective-permute-start | bytes 2654216 | tf_op jit(solution)/shard_map/ppermute | solution.py:175
  173.7 25.4 %copy-start.44 = (f32[2,768]{1,0:T(2,128)S(1)}, f32[2,768]{1,0:T(2,128)}, u32[]{:S(2)}) copy-start(f32[2,768]{1,0:T(2,128)} %param.24) | copy-start | bytes 18436
  178.8 21.4 %copy-start.25 = (f32[1200]{0:T(1024)}, f32[1200]{0:T(1024)S(1)}, u32[]{:S(2)}) copy-start(f32[1200]{0:T(1024)S(1)} %convolution_reduce_fusion) | copy-start | bytes 14404
  199.1 31.7 %copy-start.45 = (f32[768]{0:T(1024)}, f32[768]{0:T(1024)S(1)}, u32[]{:S(2)}) copy-start(f32[768]{0:T(1024)S(1)} %get-tuple-element.24) | copy-start | bytes 9220
  199.1 78.9 %copy-start.34 = (f32[768]{0:T(1024)}, f32[768]{0:T(1024)S(1)}, u32[]{:S(2)}) copy-start(f32[768]{0:T(1024)S(1)} %get-tuple-element.23) | copy-start | bytes 9220
  200.2 26.5 %all-to-all-start.1 = ((bf16[8,72,768]{2,1,0:T(8,128)(2,1)}), bf16[8,72,768]{2,1,0:T(8,128)(2,1)S(1)}, u32[]{:S(2)}, u32[]{:S(2)}) async-start(bf16[8,72,768]{2,1,0:T(8,128)(2,1)} %bitcast.21), calls=%async_computation.1 | async-start | bytes 1769472 | tf_op jit(solution)/shard_map/all_to_all | solution.py:179
  203.7 335.7 %reduce-scatter.5.cloned.1.call-start = ((), (), s32[]{:S(2)}) async-start(), calls=%async_computation.11 | async-start | bytes 5898240 | tf_op jit(solution)/shard_map/reduce_scatter | solution.py:226
  230.8 47.2 %copy-start.31 = (f32[1200]{0:T(1024)}, f32[1200]{0:T(1024)S(1)}, u32[]{:S(2)}) copy-start(f32[1200]{0:T(1024)S(1)} %add_rsqrt_fusion) | copy-start | bytes 14404
  250.1 289.3 %reduce-scatter.3.cloned.1.call-start = ((), (), s32[]{:S(2)}) async-start(), calls=%async_computation.10 | async-start | bytes 5898240 | tf_op jit(solution)/shard_map/reduce_scatter | solution.py:225
  312.0 38.0 %copy-start.13 = (bf16[8,72,768]{2,1,0:T(8,128)(2,1)}, bf16[8,72,768]{2,1,0:T(8,128)(2,1)S(1)}, u32[]{:S(2)}) copy-start(bf16[8,72,768]{2,1,0:T(8,128)(2,1)S(1)} %all_to_all.41) | copy-start | bytes 2654212
  312.0 23.2 %collective-permute-start.3 = (bf16[576,768]{1,0:T(8,128)(2,1)S(1)}, bf16[576,768]{1,0:T(8,128)(2,1)S(1)}, u32[]{:S(2)}, u32[]{:S(2)}) collective-permute-start(bf16[576,768]{1,0:T(8,128)(2,1)S(1)} %bitcast.214), channel_id=1, source_target_pairs={{0,2},{1,3},{2,0},{3,1},{4,6},{5,7},{6,4},{7,5},{8,10},{9,11},{10,... | collective-permute-start | bytes 2654216 | tf_op jit(solution)/shard_map/ppermute | solution.py:230
  336.6 13.4 %collective-permute-start.4 = (bf16[1152,768]{1,0:T(8,128)(2,1)}, bf16[1152,768]{1,0:T(8,128)(2,1)}, u32[]{:S(2)}, u32[]{:S(2)}) collective-permute-start(bf16[1152,768]{1,0:T(8,128)(2,1)} %pad_maximum_fusion.2), channel_id=1, source_target_pairs={{0,1},{1,0},{2,3},{3,2},{4,5},{5,4},{6,7},{7,6},{8,9},{9,8},{10,11... | collective-permute-start | bytes 5308424 | tf_op jit(solution)/shard_map/ppermute | solution.py:231
  396.9 20.9 %copy-start.49 = (f32[768]{0:T(1024)S(1)}, f32[768]{0:T(1024)}, u32[]{:S(2)}) copy-start(f32[768]{0:T(1024)} %all-reduce.4) | copy-start | bytes 9220
  417.3 58.1 %collective-permute-start.5 = (bf16[1152,768]{1,0:T(8,128)(2,1)}, bf16[1152,768]{1,0:T(8,128)(2,1)}, u32[]{:S(2)}, u32[]{:S(2)}) collective-permute-start(bf16[1152,768]{1,0:T(8,128)(2,1)} %slice.288), channel_id=1, source_target_pairs={{0,1},{1,0},{2,3},{3,2},{4,5},{5,4},{6,7},{7,6},{8,9},{9,8},{10,11... | collective-permute-start | bytes 5308424 | tf_op jit(solution)/shard_map/ppermute | solution.py:173
  431.0 17.2 %all-to-all-start.2 = ((bf16[4,576,192]{1,2,0:T(8,128)(2,1)}), bf16[4,576,192]{1,2,0:T(8,128)(2,1)S(1)}, u32[]{:S(2)}, u32[]{:S(2)}) async-start(bf16[4,576,192]{1,2,0:T(8,128)(2,1)} %bitcast.29), calls=%async_computation.2 | async-start | bytes 1966080 | tf_op jit(solution)/shard_map/all_to_all | solution.py:262
  436.2 19.8 %copy-start.26 = (f32[1200]{0:T(1024)S(1)}, f32[1200]{0:T(1024)}, u32[]{:S(2)}) copy-start(f32[1200]{0:T(1024)} %copy-done.25) | copy-start | bytes 14404
  448.2 18.1 %all-to-all-start.3 = ((bf16[4,624,192]{1,2,0:T(8,128)(2,1)}), bf16[4,624,192]{1,2,0:T(8,128)(2,1)}, u32[]{:S(2)}, u32[]{:S(2)}) async-start(bf16[4,624,192]{1,2,0:T(8,128)(2,1)} %bitcast.31), calls=%async_computation.3 | async-start | bytes 1966080 | tf_op jit(solution)/shard_map/all_to_all | solution.py:262
  466.3 39.6 %all-to-all-start.7 = ((bf16[4,624,192]{1,2,0:T(8,128)(2,1)}), bf16[4,624,192]{1,2,0:T(8,128)(2,1)S(1)}, u32[]{:S(2)}, u32[]{:S(2)}) async-start(bf16[4,624,192]{1,2,0:T(8,128)(2,1)} %bitcast.213), calls=%async_computation.7 | async-start | bytes 1966080 | tf_op jit(solution)/shard_map/all_to_all | solution.py:262
  481.0 22.2 %collective-permute-start.6 = (bf16[576,768]{1,0:T(8,128)(2,1)}, bf16[576,768]{1,0:T(8,128)(2,1)S(1)}, u32[]{:S(2)}, u32[]{:S(2)}) collective-permute-start(bf16[576,768]{1,0:T(8,128)(2,1)} %slice.291), channel_id=1, source_target_pairs={{0,2},{1,3},{2,0},{3,1},{4,6},{5,7},{6,4},{7,5},{8,10},{9,11},{10,... | collective-permute-start | bytes 2654216 | tf_op jit(solution)/shard_map/ppermute | solution.py:175
  505.9 30.7 %all-to-all-start.5 = ((bf16[8,72,768]{2,1,0:T(8,128)(2,1)}), bf16[8,72,768]{2,1,0:T(8,128)(2,1)S(1)}, u32[]{:S(2)}, u32[]{:S(2)}) async-start(bf16[8,72,768]{2,1,0:T(8,128)(2,1)} %bitcast.218), calls=%async_computation.5 | async-start | bytes 1769472 | tf_op jit(solution)/shard_map/all_to_all | solution.py:179
  510.6 172.1 %all-reduce.8.cloned.1.call-start = ((), (), s32[]{:S(2)}) async-start(), calls=%async_computation.14 | async-start | bytes 7077888 | tf_op jit(solution)/shard_map/psum | solution.py:250
  543.3 88.0 %all-to-all-start.6 = ((bf16[4,576,192]{1,2,0:T(8,128)(2,1)}), bf16[4,576,192]{1,2,0:T(8,128)(2,1)S(1)}, u32[]{:S(2)}, u32[]{:S(2)}) async-start(bf16[4,576,192]{1,2,0:T(8,128)(2,1)} %bitcast.43), calls=%async_computation.6 | async-start | bytes 1966080 | tf_op jit(solution)/shard_map/all_to_all | solution.py:262
  (46 other events, 388.7 us)
Sparse Core Ops, SparseCore 0:
  80.8 36.5 all-gather.7
  150.1 55.4 all-gather.9
  250.2 47.7 reduce-scatter.4
  350.1 46.8 reduce-scatter.2
  539.6 143.0 all-reduce.7
